TPU v7x, 256 devices: a whole 4x4x8 slice. The times are simulated.
256 devices in a mesh: row: 16 (over z, core), col: 16 (over x, y).
Axes of the slice: x: 4, y: 4, z: 8, core: 2. Of those that a mesh axis runs over, the one named last changes fastest.
Arguments:
- term_images: float32 [8, 4096, 4096], P(None, 'row', 'col'), may hold values from -6 to 6
- blur_width: float32 [8], replicated, may hold values from 0.8 to 6
- blur_coef: float32 [8], replicated, may hold values from -4 to 4
- direct_coef: float32 [8], replicated, may hold values from -1 to 1
- long_weight: float32 [8], replicated, may hold values from 0.2 to 2
- long_gain: float32 [1], replicated, may hold values from 0.5 to 1.5
- long_width: float32 [1], replicated, may hold values from 0.25 to 0.6
Outputs:
- resist_signal: float32 [4096, 4096], P('row', 'col')
All inputs are finite; a program needn't handle non-finite values.
Results may differ from a plain program's by a relative error of at most 0.00002.
Values sent between devices are 32-bit elements; how exact they have to be, the bound alone decides.
No kernel may reach another device: no remote copies, remote signals or barrier semaphores. Data moves between devices by JAX's collectives and lax.ppermute only.
A program may use at most 64 MiB of HBM per device.

v0:
```python
import jax
import jax.numpy as jnp
from jax import lax
from jax.sharding import PartitionSpec as P

REACH = 16
LEVELS = 5
RC = 8
BINOMIAL = (0.0625, 0.25, 0.375, 0.25, 0.0625)


def padded_2(cells, sides, width):
    for axis, dim in sides:
        count = lax.axis_size(axis)
        ends = count - 1
        head = lax.slice_in_dim(cells, 0, width, axis=dim)
        tail = lax.slice_in_dim(cells, cells.shape[dim] - width, cells.shape[dim], axis=dim)
        cells = jnp.concatenate(
            [
                lax.ppermute(tail, axis, [(i, (i + 1) % count) for i in range(ends)]),
                cells,
                lax.ppermute(head, axis, [((i + 1) % count, i) for i in range(ends)]),
            ],
            axis=dim,
        )
    return cells


def gauss_kernel(width, reach):
    offsets = jnp.arange(-reach, reach + 1).astype(jnp.float32)
    values = jnp.exp(-offsets * offsets / (2.0 * width[..., None] * width[..., None]))
    return values / jnp.sum(values, axis=-1, keepdims=True)


def down_pad(values, margin):
    return padded_2(values, (("row", 0), ("col", 1)), margin)


def up_pad(values, margin):
    return padded_2(values, (("row", 0), ("col", 1)), margin)


def coarse_pad(values, margin):
    return padded_2(values, (("row", 0), ("col", 1)), margin)


def coarsen(values, padder):
    row_count, col_count = values.shape
    padded = padder(values, 2)
    across = BINOMIAL[0] * padded[0:row_count, :]
    for tap_index in range(1, 5):
        across = across + BINOMIAL[tap_index] * padded[tap_index : tap_index + row_count, :]
    total = BINOMIAL[0] * across[:, 0:col_count]
    for tap_index in range(1, 5):
        total = total + BINOMIAL[tap_index] * across[:, tap_index : tap_index + col_count]
    return total[::2, ::2]


def refine(values, padder):
    row_count, col_count = values.shape
    padded = padder(values, 1)
    even_part = (padded[:-2] + 6.0 * padded[1:-1] + padded[2:]) * 0.125
    odd_part = (padded[1:-1] + padded[2:]) * 0.5
    rows_done = jnp.stack([even_part, odd_part], 1).reshape(2 * row_count, col_count + 2)
    even_part = (rows_done[:, :-2] + 6.0 * rows_done[:, 1:-1] + rows_done[:, 2:]) * 0.125
    odd_part = (rows_done[:, 1:-1] + rows_done[:, 2:]) * 0.5
    return jnp.stack([even_part, odd_part], 2).reshape(2 * row_count, 2 * col_count)


def coarse_blur(values, kernel, padder):
    row_count, col_count = values.shape
    padded = padder(values, RC)
    across = kernel[0] * padded[0:row_count, :]
    for tap_index in range(1, 2 * RC + 1):
        across = across + kernel[tap_index] * padded[tap_index : tap_index + row_count, :]
    total = kernel[0] * across[:, 0:col_count]
    for tap_index in range(1, 2 * RC + 1):
        total = total + kernel[tap_index] * across[:, tap_index : tap_index + col_count]
    return total


def taps_along(padded, kernel, axis, count):
    weights = kernel[:, :, None, None]
    total = weights[:, 0] * lax.slice_in_dim(padded, 0, count, axis=axis)
    for tap_index in range(1, 2 * REACH + 1):
        total = total + weights[:, tap_index] * lax.slice_in_dim(
            padded, tap_index, tap_index + count, axis=axis
        )
    return total


def on_device(term_images, blur_width, blur_coef, direct_coef, long_weight, long_gain, long_width):
    kernels = gauss_kernel(blur_width, REACH)
    tile_rows = term_images.shape[1]
    strips = lax.all_to_all(term_images, "col", split_axis=1, concat_axis=2, tiled=True)
    width_all = strips.shape[2]
    padded = jnp.pad(strips, ((0, 0), (0, 0), (REACH, REACH)))
    across_strips = taps_along(padded, kernels, 2, width_all)
    across = lax.all_to_all(across_strips, "col", split_axis=2, concat_axis=1, tiled=True)
    padded = padded_2(across, (("row", 1),), REACH)
    blurred = taps_along(padded, kernels, 1, tile_rows)
    local = jnp.sum(
        blur_coef[:, None, None] * blurred + direct_coef[:, None, None] * term_images, axis=0
    )
    source = jnp.sum(long_weight[:, None, None] * term_images * term_images, axis=0)
    coarse_kernel = gauss_kernel(long_width * RC, RC)[0]
    level_now = source
    for level_index in range(LEVELS):
        level_now = coarsen(level_now, down_pad)
    level_now = coarse_blur(level_now, coarse_kernel, coarse_pad)
    for level_index in range(LEVELS):
        level_now = refine(level_now, up_pad)
    return local + long_gain[0] * level_now


def solution(mesh):
    placed = (P(None, "row", "col"), P(), P(), P(), P(), P(), P())
    return jax.shard_map(
        on_device, mesh=mesh, in_specs=placed, out_specs=P("row", "col"), check_vma=False
    )
```

profile of v0, /device:TPU:134, one launch (start us, length us, event | category | flops | bytes accessed | tf_op | source)
XLA Modules:
  0.0 423.5 jit_solution(17075108637412598557)
XLA Ops:
  0.0 2.0 fusion
  4.0 2.4 collective-permute-start.2
  6.4 3.7 collective-permute-done.2
  10.2 5.2 %collective-permute-start.5 = (f32[260,2]{1,0:T(8,128)S(1)}, f32[260,2]{1,0:T(8,128)S(1)}, u32[]{:S(2)}, u32[]{:S(2)}) collective-permute-start(f32[260,2]{1,0:T(8,128)S(1)} %get-tuple-element.8), channel_id=1, source_target_pairs={{1,0},{2,1},{3,2},{4,3},{5,4},{6,5},{7,6},{8,7},{9,8},{10,9},{11,1... | collective-permute-start | bytes 6248 | tf_op jit(solution)/shard_map/ppermute | solution.py:22
  17.4 2.6 copy.171
  19.9 8.1 %all-to-all-start = ((f32[8,256,256]{2,0,1:T(8,128)}), f32[8,256,256]{2,0,1:T(8,128)}, u32[]{:S(2)}, u32[]{:S(2)}) async-start(f32[8,256,256]{2,0,1:T(8,128)} %copy.171), calls=%async_computation | async-start | bytes 4194304 | tf_op jit(solution)/shard_map/all_to_all | solution.py:95
  28.8 2.2 slice.1083
  33.0 2.4 collective-permute-start.6
  35.4 3.7 collective-permute-done.6
  39.2 4.9 %collective-permute-start.9 = (f32[132,2]{1,0:T(8,128)S(1)}, f32[132,2]{1,0:T(8,128)S(1)}, u32[]{:S(2)}, u32[]{:S(2)}) collective-permute-start(f32[132,2]{1,0:T(8,128)S(1)} %get-tuple-element.22), channel_id=1, source_target_pairs={{1,0},{2,1},{3,2},{4,3},{5,4},{6,5},{7,6},{8,7},{9,8},{10,9},{11,1... | collective-permute-start | bytes 3176 | tf_op jit(solution)/shard_map/ppermute | solution.py:22
  46.0 6.9 %collective-permute-done.9 = f32[132,2]{1,0:T(8,128)S(1)} collective-permute-done((f32[132,2]{1,0:T(8,128)S(1)}, f32[132,2]{1,0:T(8,128)S(1)}, u32[]{:S(2)}, u32[]{:S(2)}) %collective-permute-start.9) | collective-permute-done | bytes 1088 | tf_op jit(solution)/shard_map/ppermute | solution.py:22
  54.9 2.3 collective-permute-start.11
  57.3 2.0 collective-permute-start.10
  59.5 3.9 collective-permute-done.10
  63.5 6.6 %collective-permute-start.13 = (f32[68,2]{1,0:T(8,128)S(1)}, f32[68,2]{1,0:T(8,128)S(1)}, u32[]{:S(2)}, u32[]{:S(2)}) collective-permute-start(f32[68,2]{1,0:T(8,128)S(1)} %get-tuple-element.34), channel_id=1, source_target_pairs={{1,0},{2,1},{3,2},{4,3},{5,4},{6,5},{7,6},{8,7},{9,8},{10,9},{11,1... | collective-permute-start | bytes 1640 | tf_op jit(solution)/shard_map/ppermute | solution.py:22
  72.1 5.9 %collective-permute-done.12 = f32[68,2]{1,0:T(8,128)S(1)} collective-permute-done((f32[68,2]{1,0:T(8,128)S(1)}, f32[68,2]{1,0:T(8,128)S(1)}, u32[]{:S(2)}, u32[]{:S(2)}) %collective-permute-start.12) | collective-permute-done | bytes 576 | tf_op jit(solution)/shard_map/ppermute | solution.py:20
  80.4 2.4 collective-permute-start.14
  83.5 3.0 collective-permute-done.14
  88.5 3.9 collective-permute-start.16
  92.5 3.8 collective-permute-done.16
  98.6 2.4 collective-permute-start.18
  101.0 3.7 collective-permute-done.18
  106.7 3.9 collective-permute-start.20
  111.2 3.1 collective-permute-done.20
  114.6 1.9 collective-permute-start.23
  116.6 2.4 collective-permute-start.22
  119.6 3.1 collective-permute-done.22
  124.6 3.9 collective-permute-start.24
  129.3 3.1 collective-permute-done.24
  132.4 10.6 %fusion.192 = f32[8,24]{1,0:T(8,128)S(1)} fusion(f32[24,24]{1,0:T(8,128)S(1)} %pad_maximum_fusion.23, f32[]{:T(128)} %bitcast.59, f32[]{:T(128)} %bitcast.58, f32[]{:T(128)} %bitcast.57, f32[]{:T(128)} %bitcast.56, f32[]{:T(128)} %bitcast.55, f32[]{:T(128)} %bitcast.54, f32[]{:T(128)} %bitcast.53, f32[]{:T(128)} %bitcast.52, f32[]{:T(128)} %bitcast.51, ...), kind=kLoop, calls=%fused_computation.380 | loop fusion | flops 6336 | bytes 13892 | tf_op jit(solution)/shard_map/add | solution.py:75
  143.0 10.7 %multiply_add_fusion.1 = f32[8,8]{1,0:T(8,128)S(1)} fusion(f32[8,24]{1,0:T(8,128)S(1)} %fusion.192, f32[]{:T(128)} %bitcast.59, f32[]{:T(128)} %bitcast.58, f32[]{:T(128)} %bitcast.57, f32[]{:T(128)} %bitcast.56, f32[]{:T(128)} %bitcast.55, f32[]{:T(128)} %bitcast.54, f32[]{:T(128)} %bitcast.53, f32[]{:T(128)} %bitcast.52, f32[]{:T(128)} %bitcast.51, ...), kind=kLoop, calls=%fused_computation.413 | loop fusion | flops 2112 | bytes 4676 | tf_op jit(solution)/shard_map/add | solution.py:78
  153.8 1.9 collective-permute-start.27
  155.7 2.4 collective-permute-start.26
  158.1 3.7 collective-permute-done.26
  163.8 3.9 collective-permute-start.28
  167.7 3.7 collective-permute-done.28
  174.2 2.4 collective-permute-start.30
  176.6 3.7 collective-permute-done.30
  182.4 3.9 collective-permute-start.32
  186.3 3.6 collective-permute-done.32
  192.6 4.9 %collective-permute-start.35 = (f32[1,32]{0,1:T(8,128)S(1)}, f32[1,32]{0,1:T(8,128)S(1)}, u32[]{:S(2)}, u32[]{:S(2)}) collective-permute-start(f32[1,32]{0,1:T(8,128)S(1)} %slice.1253), channel_id=1, source_target_pairs={{16,0},{32,16},{48,32},{64,48},{80,64},{96,80},{112,96},{128,112},... | collective-permute-start | bytes 392 | tf_op jit(solution)/shard_map/ppermute | solution.py:22
  200.9 4.1 collective-permute-start.36
  205.0 3.4 collective-permute-done.36
  208.7 4.1 copy.217
  212.9 2.7 all_to_all.29
  215.6 46.7 %multiply_add_fusion = f32[8,16,4096]{2,1,0:T(8,128)} fusion(f32[8,16,4096]{2,1,0:T(8,128)} %all_to_all.29, f32[8]{0:T(128)S(1)} %get-tuple-element.48, f32[8]{0:T(128)S(1)} %get-tuple-element.49, f32[8]{0:T(128)S(1)} %get-tuple-element.50, f32[8]{0:T(128)S(1)} %get-tuple-element.51, f32[8]{0:T(128)S(1)} %get-tuple-element.52, f32[8]{0:T(128)S(1)} %get-tuple-element.53, ...), kind=kLoop, calls=%fused_computation.158 | loop fusion | flops 34078720 | bytes 4195360 | tf_op jit(solution)/shard_map/add | solution.py:86
  262.3 9.6 %copy.173 = f32[8,16,4096]{1,0,2:T(8,128)} copy(f32[8,16,4096]{2,1,0:T(8,128)} %multiply_add_fusion) | data formatting | bytes 4194304 | tf_op jit(solution)/shard_map/add | solution.py:86
  271.9 15.1 %reshape.234 = f32[16,1,32768]{2,1,0:T(1,128)} reshape(f32[4096,8,16]{2,1,0:T(8,128)} %bitcast.148) | data formatting | bytes 4194304
  287.0 4.5 %all-to-all-start.1 = ((f32[16,1,32768]{2,1,0:T(1,128)}), f32[16,1,32768]{2,1,0:T(1,128)}, u32[]{:S(2)}, u32[]{:S(2)}) async-start(f32[16,1,32768]{2,1,0:T(1,128)} %reshape.234), calls=%async_computation.1 | async-start | bytes 4194304 | tf_op jit(solution)/shard_map/all_to_all | solution.py:99
  291.8 3.5 collective-permute-start.39
  297.5 4.1 collective-permute-done.38
  301.8 4.5 %collective-permute-start.41 = (f32[66,1]{0,1:T(1,128)S(1)}, f32[66,1]{0,1:T(1,128)S(1)}, u32[]{:S(2)}, u32[]{:S(2)}) collective-permute-start(f32[66,1]{0,1:T(1,128)S(1)} %get-tuple-element.20), channel_id=1, source_target_pairs={{1,0},{2,1},{3,2},{4,3},{5,4},{6,5},{7,6},{8,7},{9,8},{10,9},{11,1... | collective-permute-start | bytes 800 | tf_op jit(solution)/shard_map/ppermute | solution.py:22
  308.2 6.6 %collective-permute-done.41 = f32[66,1]{0,1:T(1,128)S(1)} collective-permute-done((f32[66,1]{0,1:T(1,128)S(1)}, f32[66,1]{0,1:T(1,128)S(1)}, u32[]{:S(2)}, u32[]{:S(2)}) %collective-permute-start.41) | collective-permute-done | bytes 296 | tf_op jit(solution)/shard_map/ppermute | solution.py:22
  316.3 5.1 %collective-permute-start.43 = (f32[1,128]{0,1:T(8,128)S(1)}, f32[1,128]{0,1:T(8,128)S(1)}, u32[]{:S(2)}, u32[]{:S(2)}) collective-permute-start(f32[1,128]{0,1:T(8,128)S(1)} %slice.1255), channel_id=1, source_target_pairs={{16,0},{32,16},{48,32},{64,48},{80,64},{96,80},{112,96},{128,112},... | collective-permute-start | bytes 1544 | tf_op jit(solution)/shard_map/ppermute | solution.py:22
  323.6 4.1 collective-permute-done.42
  327.8 4.4 %collective-permute-start.45 = (f32[130,1]{0,1:T(1,128)S(1)}, f32[130,1]{0,1:T(1,128)S(1)}, u32[]{:S(2)}, u32[]{:S(2)}) collective-permute-start(f32[130,1]{0,1:T(1,128)S(1)} %get-tuple-element.14), channel_id=1, source_target_pairs={{1,0},{2,1},{3,2},{4,3},{5,4},{6,5},{7,6},{8,7},{9,8},{10,9},{11,1... | collective-permute-start | bytes 1568 | tf_op jit(solution)/shard_map/ppermute | solution.py:22
  332.2 2.1 collective-permute-start.44
  335.0 4.8 %collective-permute-done.44 = f32[130,1]{0,1:T(1,128)S(1)} collective-permute-done((f32[130,1]{0,1:T(1,128)S(1)}, f32[130,1]{0,1:T(1,128)S(1)}, u32[]{:S(2)}, u32[]{:S(2)}) %collective-permute-start.44) | collective-permute-done | bytes 552 | tf_op jit(solution)/shard_map/ppermute | solution.py:20
  340.9 8.6 %reduce.1 = f32[16,32768]{1,0:T(8,128)} reduce(f32[16,1,32768]{2,1,0:T(1,128)} %all-to-all-done.1, f32[]{:T(128)} %broadcast.217), dimensions={1}, to_apply=%all_to_all.30.reduce_sub_computation | reduce | bytes 4194308 | tf_op jit(solution)/shard_map/all_to_all | solution.py:99
  349.5 14.6 %reshape.235 = f32[4096,8,16]{2,1,0:T(8,128)} reshape(f32[16,32768]{1,0:T(8,128)} %reduce.1) | data formatting | bytes 4194304
  364.1 10.8 %copy.175 = f32[8,16,16,256]{3,2,1,0:T(8,128)} copy(f32[8,16,16,256]{2,0,3,1:T(8,128)} %bitcast.149) | data formatting | bytes 4194304 | tf_op jit(solution)/shard_map/all_to_all | solution.py:99
  377.9 2.7 collective-permute-start
  381.2 4.2 collective-permute-done
  385.4 37.3 %fusion.7 = f32[256,256]{1,0:T(8,128)S(1)} fusion(f32[8,16,256]{2,1,0:T(8,128)S(1)} %collective-permute-done.1, f32[8,16,256]{2,1,0:T(8,128)S(1)} %collective-permute-done, f32[8,256,256]{2,1,0:T(8,128)} %bitcast.151, f32[8,256,256]{2,1,0:T(8,128)S(1)} %copy-done, f32[8]{0:T(128)S(1)} %copy-done.1, f32[8]{0:T(128)S(1)} %get-tuple-element.48, ...), kind=kLoop, calls=%fused_computation.38 | loop fusion | flops 52887552 | bytes 4719712 | tf_op jit(solution)/shard_map/reduce_sum | solution.py:102
  (173 shorter events, 52.6 us)
Async XLA Ops:
  0.0 17.4 %copy-start = (f32[8,256,256]{2,1,0:T(8,128)S(1)}, f32[8,256,256]{2,1,0:T(8,128)}, u32[]{:S(2)}) copy-start(f32[8,256,256]{2,1,0:T(8,128)} %param.7) | copy-start | bytes 6291460
  2.1 4.3 %collective-permute-start.3 = (f32[2,256]{1,0:T(2,128)S(1)}, f32[2,256]{1,0:T(2,128)S(1)}, u32[]{:S(2)}, u32[]{:S(2)}) collective-permute-start(f32[2,256]{1,0:T(2,128)S(1)} %get-tuple-element.12), channel_id=1, source_target_pairs={{16,0},{32,16},{48,32},{64,48},{80,64},{96,80},{112,96},{128,112},... | collective-permute-start | bytes 6152 | tf_op jit(solution)/shard_map/ppermute | solution.py:22
  4.0 6.1 %collective-permute-start.2 = (f32[2,256]{1,0:T(2,128)S(1)}, f32[2,256]{1,0:T(2,128)S(1)}, u32[]{:S(2)}, u32[]{:S(2)}) collective-permute-start(f32[2,256]{1,0:T(2,128)S(1)} %get-tuple-element.11), channel_id=1, source_target_pairs={{0,16},{16,32},{32,48},{48,64},{64,80},{80,96},{96,112},{112,128},... | collective-permute-start | bytes 6152 | tf_op jit(solution)/shard_map/ppermute | solution.py:20
  10.2 17.8 %collective-permute-start.5 = (f32[260,2]{1,0:T(8,128)S(1)}, f32[260,2]{1,0:T(8,128)S(1)}, u32[]{:S(2)}, u32[]{:S(2)}) collective-permute-start(f32[260,2]{1,0:T(8,128)S(1)} %get-tuple-element.8), channel_id=1, source_target_pairs={{1,0},{2,1},{3,2},{4,3},{5,4},{6,5},{7,6},{8,7},{9,8},{10,9},{11,1... | collective-permute-start | bytes 6248 | tf_op jit(solution)/shard_map/ppermute | solution.py:22
  15.4 12.6 %collective-permute-start.4 = (f32[260,2]{1,0:T(8,128)S(1)}, f32[260,2]{1,0:T(8,128)S(1)}, u32[]{:S(2)}, u32[]{:S(2)}) collective-permute-start(f32[260,2]{1,0:T(8,128)S(1)} %get-tuple-element.7), channel_id=1, source_target_pairs={{0,1},{1,2},{2,3},{3,4},{4,5},{5,6},{6,7},{7,8},{8,9},{9,10},{10,1... | collective-permute-start | bytes 6248 | tf_op jit(solution)/shard_map/ppermute | solution.py:20
  19.9 188.8 %all-to-all-start = ((f32[8,256,256]{2,0,1:T(8,128)}), f32[8,256,256]{2,0,1:T(8,128)}, u32[]{:S(2)}, u32[]{:S(2)}) async-start(f32[8,256,256]{2,0,1:T(8,128)} %copy.171), calls=%async_computation | async-start | bytes 4194304 | tf_op jit(solution)/shard_map/all_to_all | solution.py:95
  28.2 7.2 %copy-start.3 = (f32[8]{0:T(128)S(1)}, f32[8]{0:T(128)}, u32[]{:S(2)}) copy-start(f32[8]{0:T(128)} %param.8) | copy-start | bytes 100
  31.1 4.4 %collective-permute-start.7 = (f32[2,128]{1,0:T(2,128)S(1)}, f32[2,128]{1,0:T(2,128)S(1)}, u32[]{:S(2)}, u32[]{:S(2)}) collective-permute-start(f32[2,128]{1,0:T(2,128)S(1)} %get-tuple-element.28), channel_id=1, source_target_pairs={{16,0},{32,16},{48,32},{64,48},{80,64},{96,80},{112,96},{128,112},... | collective-permute-start | bytes 3080 | tf_op jit(solution)/shard_map/ppermute | solution.py:22
  33.0 6.1 %collective-permute-start.6 = (f32[2,128]{1,0:T(2,128)S(1)}, f32[2,128]{1,0:T(2,128)S(1)}, u32[]{:S(2)}, u32[]{:S(2)}) collective-permute-start(f32[2,128]{1,0:T(2,128)S(1)} %get-tuple-element.27), channel_id=1, source_target_pairs={{0,16},{16,32},{32,48},{48,64},{64,80},{80,96},{96,112},{112,128},... | collective-permute-start | bytes 3080 | tf_op jit(solution)/shard_map/ppermute | solution.py:20
  39.2 13.7 %collective-permute-start.9 = (f32[132,2]{1,0:T(8,128)S(1)}, f32[132,2]{1,0:T(8,128)S(1)}, u32[]{:S(2)}, u32[]{:S(2)}) collective-permute-start(f32[132,2]{1,0:T(8,128)S(1)} %get-tuple-element.22), channel_id=1, source_target_pairs={{1,0},{2,1},{3,2},{4,3},{5,4},{6,5},{7,6},{8,7},{9,8},{10,9},{11,1... | collective-permute-start | bytes 3176 | tf_op jit(solution)/shard_map/ppermute | solution.py:22
  44.1 9.9 %collective-permute-start.8 = (f32[132,2]{1,0:T(8,128)S(1)}, f32[132,2]{1,0:T(8,128)S(1)}, u32[]{:S(2)}, u32[]{:S(2)}) collective-permute-start(f32[132,2]{1,0:T(8,128)S(1)} %get-tuple-element.21), channel_id=1, source_target_pairs={{0,1},{1,2},{2,3},{3,4},{4,5},{5,6},{6,7},{7,8},{8,9},{9,10},{10,1... | collective-permute-start | bytes 3176 | tf_op jit(solution)/shard_map/ppermute | solution.py:20
  54.9 4.5 %collective-permute-start.11 = (f32[2,64]{1,0:T(2,128)S(1)}, f32[2,64]{1,0:T(2,128)S(1)}, u32[]{:S(2)}, u32[]{:S(2)}) collective-permute-start(f32[2,64]{1,0:T(2,128)S(1)} %get-tuple-element.40), channel_id=1, source_target_pairs={{16,0},{32,16},{48,32},{64,48},{80,64},{96,80},{112,96},{128,112},... | collective-permute-start | bytes 1544 | tf_op jit(solution)/shard_map/ppermute | solution.py:22
  57.3 6.1 %collective-permute-start.10 = (f32[2,64]{1,0:T(2,128)S(1)}, f32[2,64]{1,0:T(2,128)S(1)}, u32[]{:S(2)}, u32[]{:S(2)}) collective-permute-start(f32[2,64]{1,0:T(2,128)S(1)} %get-tuple-element.39), channel_id=1, source_target_pairs={{0,16},{16,32},{32,48},{48,64},{64,80},{80,96},{96,112},{112,128},... | collective-permute-start | bytes 1544 | tf_op jit(solution)/shard_map/ppermute | solution.py:20
  63.5 8.7 %collective-permute-start.13 = (f32[68,2]{1,0:T(8,128)S(1)}, f32[68,2]{1,0:T(8,128)S(1)}, u32[]{:S(2)}, u32[]{:S(2)}) collective-permute-start(f32[68,2]{1,0:T(8,128)S(1)} %get-tuple-element.34), channel_id=1, source_target_pairs={{1,0},{2,1},{3,2},{4,3},{5,4},{6,5},{7,6},{8,7},{9,8},{10,9},{11,1... | collective-permute-start | bytes 1640 | tf_op jit(solution)/shard_map/ppermute | solution.py:22
  70.1 8.0 %collective-permute-start.12 = (f32[68,2]{1,0:T(8,128)S(1)}, f32[68,2]{1,0:T(8,128)S(1)}, u32[]{:S(2)}, u32[]{:S(2)}) collective-permute-start(f32[68,2]{1,0:T(8,128)S(1)} %get-tuple-element.33), channel_id=1, source_target_pairs={{0,1},{1,2},{2,3},{3,4},{4,5},{5,6},{6,7},{7,8},{8,9},{9,10},{10,1... | collective-permute-start | bytes 1640 | tf_op jit(solution)/shard_map/ppermute | solution.py:20
  78.5 5.0 %collective-permute-start.15 = (f32[2,32]{1,0:T(2,128)S(1)}, f32[2,32]{1,0:T(2,128)S(1)}, u32[]{:S(2)}, u32[]{:S(2)}) collective-permute-start(f32[2,32]{1,0:T(2,128)S(1)} %get-tuple-element.83), channel_id=1, source_target_pairs={{16,0},{32,16},{48,32},{64,48},{80,64},{96,80},{112,96},{128,112},... | collective-permute-start | bytes 776 | tf_op jit(solution)/shard_map/ppermute | solution.py:22
  80.4 6.1 %collective-permute-start.14 = (f32[2,32]{1,0:T(2,128)S(1)}, f32[2,32]{1,0:T(2,128)S(1)}, u32[]{:S(2)}, u32[]{:S(2)}) collective-permute-start(f32[2,32]{1,0:T(2,128)S(1)} %get-tuple-element.82), channel_id=1, source_target_pairs={{0,16},{16,32},{32,48},{48,64},{64,80},{80,96},{96,112},{112,128},... | collective-permute-start | bytes 776 | tf_op jit(solution)/shard_map/ppermute | solution.py:20
  86.6 5.9 %collective-permute-start.17 = (f32[36,2]{1,0:T(8,128)S(1)}, f32[36,2]{1,0:T(8,128)S(1)}, u32[]{:S(2)}, u32[]{:S(2)}) collective-permute-start(f32[36,2]{1,0:T(8,128)S(1)} %get-tuple-element.46), channel_id=1, source_target_pairs={{1,0},{2,1},{3,2},{4,3},{5,4},{6,5},{7,6},{8,7},{9,8},{10,9},{11,1... | collective-permute-start | bytes 872 | tf_op jit(solution)/shard_map/ppermute | solution.py:22
  88.5 7.8 %collective-permute-start.16 = (f32[36,2]{1,0:T(8,128)S(1)}, f32[36,2]{1,0:T(8,128)S(1)}, u32[]{:S(2)}, u32[]{:S(2)}) collective-permute-start(f32[36,2]{1,0:T(8,128)S(1)} %get-tuple-element.45), channel_id=1, source_target_pairs={{0,1},{1,2},{2,3},{3,4},{4,5},{5,6},{6,7},{7,8},{8,9},{9,10},{10,1... | collective-permute-start | bytes 872 | tf_op jit(solution)/shard_map/ppermute | solution.py:20
  96.6 4.4 %collective-permute-start.19 = (f32[2,16]{1,0:T(2,128)S(1)}, f32[2,16]{1,0:T(2,128)S(1)}, u32[]{:S(2)}, u32[]{:S(2)}) collective-permute-start(f32[2,16]{1,0:T(2,128)S(1)} %get-tuple-element.97), channel_id=1, source_target_pairs={{16,0},{32,16},{48,32},{64,48},{80,64},{96,80},{112,96},{128,112},... | collective-permute-start | bytes 392 | tf_op jit(solution)/shard_map/ppermute | solution.py:22
  98.6 6.1 %collective-permute-start.18 = (f32[2,16]{1,0:T(2,128)S(1)}, f32[2,16]{1,0:T(2,128)S(1)}, u32[]{:S(2)}, u32[]{:S(2)}) collective-permute-start(f32[2,16]{1,0:T(2,128)S(1)} %get-tuple-element.96), channel_id=1, source_target_pairs={{0,16},{16,32},{32,48},{48,64},{64,80},{80,96},{96,112},{112,128},... | collective-permute-start | bytes 392 | tf_op jit(solution)/shard_map/ppermute | solution.py:20
  104.8 6.5 %collective-permute-start.21 = (f32[20,2]{1,0:T(8,128)S(1)}, f32[20,2]{1,0:T(8,128)S(1)}, u32[]{:S(2)}, u32[]{:S(2)}) collective-permute-start(f32[20,2]{1,0:T(8,128)S(1)} %get-tuple-element.87), channel_id=1, source_target_pairs={{1,0},{2,1},{3,2},{4,3},{5,4},{6,5},{7,6},{8,7},{9,8},{10,9},{11,1... | collective-permute-start | bytes 488 | tf_op jit(solution)/shard_map/ppermute | solution.py:22
  106.7 7.7 %collective-permute-start.20 = (f32[20,2]{1,0:T(8,128)S(1)}, f32[20,2]{1,0:T(8,128)S(1)}, u32[]{:S(2)}, u32[]{:S(2)}) collective-permute-start(f32[20,2]{1,0:T(8,128)S(1)} %get-tuple-element.86), channel_id=1, source_target_pairs={{0,1},{1,2},{2,3},{3,4},{4,5},{5,6},{6,7},{7,8},{8,9},{9,10},{10,1... | collective-permute-start | bytes 488 | tf_op jit(solution)/shard_map/ppermute | solution.py:20
  114.6 4.9 %collective-permute-start.23 = (f32[8,8]{1,0:T(8,128)S(1)}, f32[8,8]{1,0:T(8,128)S(1)}, u32[]{:S(2)}, u32[]{:S(2)}) collective-permute-start(f32[8,8]{1,0:T(8,128)S(1)} %slice.1143), channel_id=1, source_target_pairs={{16,0},{32,16},{48,32},{64,48},{80,64},{96,80},{112,96},{128,112},... | collective-permute-start | bytes 776 | tf_op jit(solution)/shard_map/ppermute | solution.py:22
  116.6 6.1 %collective-permute-start.22 = (f32[8,8]{1,0:T(8,128)S(1)}, f32[8,8]{1,0:T(8,128)S(1)}, u32[]{:S(2)}, u32[]{:S(2)}) collective-permute-start(f32[8,8]{1,0:T(8,128)S(1)} %slice.1143), channel_id=1, source_target_pairs={{0,16},{16,32},{32,48},{48,64},{64,80},{80,96},{96,112},{112,128},... | collective-permute-start | bytes 776 | tf_op jit(solution)/shard_map/ppermute | solution.py:20
  122.7 6.6 %collective-permute-start.25 = (f32[24,8]{1,0:T(8,128)S(1)}, f32[24,8]{1,0:T(8,128)S(1)}, u32[]{:S(2)}, u32[]{:S(2)}) collective-permute-start(f32[24,8]{1,0:T(8,128)S(1)} %pad_maximum_fusion.22), channel_id=1, source_target_pairs={{1,0},{2,1},{3,2},{4,3},{5,4},{6,5},{7,6},{8,7},{9,8},{10,9},{11,1... | collective-permute-start | bytes 2312 | tf_op jit(solution)/shard_map/ppermute | solution.py:22
  124.6 7.7 %collective-permute-start.24 = (f32[24,8]{1,0:T(8,128)S(1)}, f32[24,8]{1,0:T(8,128)S(1)}, u32[]{:S(2)}, u32[]{:S(2)}) collective-permute-start(f32[24,8]{1,0:T(8,128)S(1)} %pad_maximum_fusion.22), channel_id=1, source_target_pairs={{0,1},{1,2},{2,3},{3,4},{4,5},{5,6},{6,7},{7,8},{8,9},{9,10},{10,1... | collective-permute-start | bytes 2312 | tf_op jit(solution)/shard_map/ppermute | solution.py:20
  153.8 4.3 %collective-permute-start.27 = (f32[1,8]{1,0:T(1,128)S(1)}, f32[1,8]{1,0:T(1,128)S(1)}, u32[]{:S(2)}, u32[]{:S(2)}) collective-permute-start(f32[1,8]{1,0:T(1,128)S(1)} %get-tuple-element.99), channel_id=1, source_target_pairs={{16,0},{32,16},{48,32},{64,48},{80,64},{96,80},{112,96},{128,112},... | collective-permute-start | bytes 104 | tf_op jit(solution)/shard_map/ppermute | solution.py:22
  155.7 6.1 %collective-permute-start.26 = (f32[1,8]{1,0:T(1,128)S(1)}, f32[1,8]{1,0:T(1,128)S(1)}, u32[]{:S(2)}, u32[]{:S(2)}) collective-permute-start(f32[1,8]{1,0:T(1,128)S(1)} %get-tuple-element.98), channel_id=1, source_target_pairs={{0,16},{16,32},{32,48},{48,64},{64,80},{80,96},{96,112},{112,128},... | collective-permute-start | bytes 104 | tf_op jit(solution)/shard_map/ppermute | solution.py:20
  161.9 5.9 %collective-permute-start.29 = (f32[10,1]{1,0:T(8,128)S(1)}, f32[10,1]{1,0:T(8,128)S(1)}, u32[]{:S(2)}, u32[]{:S(2)}) collective-permute-start(f32[10,1]{1,0:T(8,128)S(1)} %get-tuple-element.95), channel_id=1, source_target_pairs={{1,0},{2,1},{3,2},{4,3},{5,4},{6,5},{7,6},{8,7},{9,8},{10,9},{11,1... | collective-permute-start | bytes 128 | tf_op jit(solution)/shard_map/ppermute | solution.py:22
  163.8 7.7 %collective-permute-start.28 = (f32[10,1]{1,0:T(8,128)S(1)}, f32[10,1]{1,0:T(8,128)S(1)}, u32[]{:S(2)}, u32[]{:S(2)}) collective-permute-start(f32[10,1]{1,0:T(8,128)S(1)} %get-tuple-element.94), channel_id=1, source_target_pairs={{0,1},{1,2},{2,3},{3,4},{4,5},{5,6},{6,7},{7,8},{8,9},{9,10},{10,1... | collective-permute-start | bytes 128 | tf_op jit(solution)/shard_map/ppermute | solution.py:20
  172.1 8.3 %collective-permute-start.31 = (f32[1,16]{0,1:T(8,128)S(1)}, f32[1,16]{0,1:T(8,128)S(1)}, u32[]{:S(2)}, u32[]{:S(2)}) collective-permute-start(f32[1,16]{0,1:T(8,128)S(1)} %slice.1252), channel_id=1, source_target_pairs={{16,0},{32,16},{48,32},{64,48},{80,64},{96,80},{112,96},{128,112},... | collective-permute-start | bytes 200 | tf_op jit(solution)/shard_map/ppermute | solution.py:22
  174.2 6.1 %collective-permute-start.30 = (f32[1,16]{1,0:T(1,128)S(1)}, f32[1,16]{1,0:T(1,128)S(1)}, u32[]{:S(2)}, u32[]{:S(2)}) collective-permute-start(f32[1,16]{1,0:T(1,128)S(1)} %slice.1205), channel_id=1, source_target_pairs={{0,16},{16,32},{32,48},{48,64},{64,80},{80,96},{96,112},{112,128},... | collective-permute-start | bytes 200 | tf_op jit(solution)/shard_map/ppermute | solution.py:20
  180.4 5.9 %collective-permute-start.33 = (f32[18,1]{0,1:T(1,128)S(1)}, f32[18,1]{0,1:T(1,128)S(1)}, u32[]{:S(2)}, u32[]{:S(2)}) collective-permute-start(f32[18,1]{0,1:T(1,128)S(1)} %get-tuple-element.42), channel_id=1, source_target_pairs={{1,0},{2,1},{3,2},{4,3},{5,4},{6,5},{7,6},{8,7},{9,8},{10,9},{11,1... | collective-permute-start | bytes 224 | tf_op jit(solution)/shard_map/ppermute | solution.py:22
  182.4 7.6 %collective-permute-start.32 = (f32[18,1]{0,1:T(1,128)S(1)}, f32[18,1]{0,1:T(1,128)S(1)}, u32[]{:S(2)}, u32[]{:S(2)}) collective-permute-start(f32[18,1]{0,1:T(1,128)S(1)} %get-tuple-element.41), channel_id=1, source_target_pairs={{0,1},{1,2},{2,3},{3,4},{4,5},{5,6},{6,7},{7,8},{8,9},{9,10},{10,1... | collective-permute-start | bytes 224 | tf_op jit(solution)/shard_map/ppermute | solution.py:20
  190.6 6.9 %collective-permute-start.34 = (f32[1,32]{1,0:T(1,128)S(1)}, f32[1,32]{1,0:T(1,128)S(1)}, u32[]{:S(2)}, u32[]{:S(2)}) collective-permute-start(f32[1,32]{1,0:T(1,128)S(1)} %slice.1217), channel_id=1, source_target_pairs={{0,16},{16,32},{32,48},{48,64},{64,80},{80,96},{96,112},{112,128},... | collective-permute-start | bytes 392 | tf_op jit(solution)/shard_map/ppermute | solution.py:20
  192.6 6.3 %collective-permute-start.35 = (f32[1,32]{0,1:T(8,128)S(1)}, f32[1,32]{0,1:T(8,128)S(1)}, u32[]{:S(2)}, u32[]{:S(2)}) collective-permute-start(f32[1,32]{0,1:T(8,128)S(1)} %slice.1253), channel_id=1, source_target_pairs={{16,0},{32,16},{48,32},{64,48},{80,64},{96,80},{112,96},{128,112},... | collective-permute-start | bytes 392 | tf_op jit(solution)/shard_map/ppermute | solution.py:22
  198.9 6.0 %collective-permute-start.37 = (f32[34,1]{0,1:T(1,128)S(1)}, f32[34,1]{0,1:T(1,128)S(1)}, u32[]{:S(2)}, u32[]{:S(2)}) collective-permute-start(f32[34,1]{0,1:T(1,128)S(1)} %get-tuple-element.30), channel_id=1, source_target_pairs={{1,0},{2,1},{3,2},{4,3},{5,4},{6,5},{7,6},{8,7},{9,8},{10,9},{11,1... | collective-permute-start | bytes 416 | tf_op jit(solution)/shard_map/ppermute | solution.py:22
  200.9 7.6 %collective-permute-start.36 = (f32[34,1]{0,1:T(1,128)S(1)}, f32[34,1]{0,1:T(1,128)S(1)}, u32[]{:S(2)}, u32[]{:S(2)}) collective-permute-start(f32[34,1]{0,1:T(1,128)S(1)} %get-tuple-element.29), channel_id=1, source_target_pairs={{0,1},{1,2},{2,3},{3,4},{4,5},{5,6},{6,7},{7,8},{8,9},{9,10},{10,1... | collective-permute-start | bytes 416 | tf_op jit(solution)/shard_map/ppermute | solution.py:20
  287.0 53.4 %all-to-all-start.1 = ((f32[16,1,32768]{2,1,0:T(1,128)}), f32[16,1,32768]{2,1,0:T(1,128)}, u32[]{:S(2)}, u32[]{:S(2)}) async-start(f32[16,1,32768]{2,1,0:T(1,128)} %reshape.234), calls=%async_computation.1 | async-start | bytes 4194304 | tf_op jit(solution)/shard_map/all_to_all | solution.py:99
  291.8 9.9 %collective-permute-start.39 = (f32[1,64]{0,1:T(8,128)S(1)}, f32[1,64]{0,1:T(8,128)S(1)}, u32[]{:S(2)}, u32[]{:S(2)}) collective-permute-start(f32[1,64]{0,1:T(8,128)S(1)} %slice.1254), channel_id=1, source_target_pairs={{16,0},{32,16},{48,32},{64,48},{80,64},{96,80},{112,96},{128,112},... | collective-permute-start | bytes 776 | tf_op jit(solution)/shard_map/ppermute | solution.py:22
  295.5 6.1 %collective-permute-start.38 = (f32[1,64]{1,0:T(1,128)S(1)}, f32[1,64]{1,0:T(1,128)S(1)}, u32[]{:S(2)}, u32[]{:S(2)}) collective-permute-start(f32[1,64]{1,0:T(1,128)S(1)} %slice.1229), channel_id=1, source_target_pairs={{0,16},{16,32},{32,48},{48,64},{64,80},{80,96},{96,112},{112,128},... | collective-permute-start | bytes 776 | tf_op jit(solution)/shard_map/ppermute | solution.py:20
  301.8 13.0 %collective-permute-start.41 = (f32[66,1]{0,1:T(1,128)S(1)}, f32[66,1]{0,1:T(1,128)S(1)}, u32[]{:S(2)}, u32[]{:S(2)}) collective-permute-start(f32[66,1]{0,1:T(1,128)S(1)} %get-tuple-element.20), channel_id=1, source_target_pairs={{1,0},{2,1},{3,2},{4,3},{5,4},{6,5},{7,6},{8,7},{9,8},{10,9},{11,1... | collective-permute-start | bytes 800 | tf_op jit(solution)/shard_map/ppermute | solution.py:22
  306.3 9.4 %collective-permute-start.40 = (f32[66,1]{0,1:T(1,128)S(1)}, f32[66,1]{0,1:T(1,128)S(1)}, u32[]{:S(2)}, u32[]{:S(2)}) collective-permute-start(f32[66,1]{0,1:T(1,128)S(1)} %get-tuple-element.19), channel_id=1, source_target_pairs={{0,1},{1,2},{2,3},{3,4},{4,5},{5,6},{6,7},{7,8},{8,9},{9,10},{10,1... | collective-permute-start | bytes 800 | tf_op jit(solution)/shard_map/ppermute | solution.py:20
  316.3 11.5 %collective-permute-start.43 = (f32[1,128]{0,1:T(8,128)S(1)}, f32[1,128]{0,1:T(8,128)S(1)}, u32[]{:S(2)}, u32[]{:S(2)}) collective-permute-start(f32[1,128]{0,1:T(8,128)S(1)} %slice.1255), channel_id=1, source_target_pairs={{16,0},{32,16},{48,32},{64,48},{80,64},{96,80},{112,96},{128,112},... | collective-permute-start | bytes 1544 | tf_op jit(solution)/shard_map/ppermute | solution.py:22
  321.6 6.1 %collective-permute-start.42 = (f32[1,128]{1,0:T(1,128)S(1)}, f32[1,128]{1,0:T(1,128)S(1)}, u32[]{:S(2)}, u32[]{:S(2)}) collective-permute-start(f32[1,128]{1,0:T(1,128)S(1)} %slice.1241), channel_id=1, source_target_pairs={{0,16},{16,32},{32,48},{48,64},{64,80},{80,96},{96,112},{112,128},... | collective-permute-start | bytes 1544 | tf_op jit(solution)/shard_map/ppermute | solution.py:20
  327.8 7.2 %collective-permute-start.45 = (f32[130,1]{0,1:T(1,128)S(1)}, f32[130,1]{0,1:T(1,128)S(1)}, u32[]{:S(2)}, u32[]{:S(2)}) collective-permute-start(f32[130,1]{0,1:T(1,128)S(1)} %get-tuple-element.14), channel_id=1, source_target_pairs={{1,0},{2,1},{3,2},{4,3},{5,4},{6,5},{7,6},{8,7},{9,8},{10,9},{11,1... | collective-permute-start | bytes 1568 | tf_op jit(solution)/shard_map/ppermute | solution.py:22
  332.2 7.6 %collective-permute-start.44 = (f32[130,1]{0,1:T(1,128)S(1)}, f32[130,1]{0,1:T(1,128)S(1)}, u32[]{:S(2)}, u32[]{:S(2)}) collective-permute-start(f32[130,1]{0,1:T(1,128)S(1)} %get-tuple-element.13), channel_id=1, source_target_pairs={{0,1},{1,2},{2,3},{3,4},{4,5},{5,6},{6,7},{7,8},{8,9},{9,10},{10,1... | collective-permute-start | bytes 1568 | tf_op jit(solution)/shard_map/ppermute | solution.py:20
  374.9 10.4 %copy-start.1 = (f32[8]{0:T(128)S(1)}, f32[8]{0:T(128)}, u32[]{:S(2)}) copy-start(f32[8]{0:T(128)} %param.10) | copy-start | bytes 100
  374.9 10.4 %copy-start.2 = (f32[8]{0:T(128)S(1)}, f32[8]{0:T(128)}, u32[]{:S(2)}) copy-start(f32[8]{0:T(128)} %param.9) | copy-start | bytes 100
  376.0 5.3 %collective-permute-start.1 = (f32[8,16,256]{2,1,0:T(8,128)S(1)}, f32[8,16,256]{2,1,0:T(8,128)S(1)}, u32[]{:S(2)}, u32[]{:S(2)}) collective-permute-start(f32[8,16,256]{2,1,0:T(8,128)S(1)} %get-tuple-element.6), channel_id=1, source_target_pairs={{16,0},{32,16},{48,32},{64,48},{80,64},{96,80},{112,96},{128,112},... | collective-permute-start | bytes 393224 | tf_op jit(solution)/shard_map/ppermute | solution.py:22
  377.9 7.5 %collective-permute-start = (f32[8,16,256]{2,1,0:T(8,128)S(1)}, f32[8,16,256]{2,1,0:T(8,128)S(1)}, u32[]{:S(2)}, u32[]{:S(2)}) collective-permute-start(f32[8,16,256]{2,1,0:T(8,128)S(1)} %get-tuple-element.5), channel_id=1, source_target_pairs={{0,16},{16,32},{32,48},{48,64},{64,80},{80,96},{96,112},{112,128},... | collective-permute-start | bytes 393224 | tf_op jit(solution)/shard_map/ppermute | solution.py:20
where the time goes:
time: 426 us; the launch traced here: 423 us
  starting transfers between devices  141 us (33%)
  other arithmetic  122 us (29%)
  waiting for transfers between devices  88.9 us (21%)
  local copies, waits for them, and re-layouts  68.9 us (16%)
    ppermute x23, waiting for transfers between devices, padded_2(): lax.ppermute(tail, axis, [(i, (i + 1) % count) for i in range(ends)])  74.1 us
    ppermute x23, starting transfers between devices, padded_2(): lax.ppermute(head, axis, [((i + 1) % count, i) for i in range(ends)])  68.1 us
    ppermute x23, starting transfers between devices, padded_2(): lax.ppermute(tail, axis, [(i, (i + 1) % count) for i in range(ends)])  60.8 us
    add x1, other arithmetic, taps_along(): total + weights[:, tap_index] * lax.slice_in_dim(padded, tap_index, tap_i...  46.7 us
    reduce_sum x1, other arithmetic, on_device(): jnp.sum(blur_coef[:, None, None] * blurred + direct_coef[:, None, None] *...  37.3 us
    unnamed x11, local copies, waits for them, and re-layouts  32.2 us
    ppermute x23, waiting for transfers between devices, padded_2(): lax.ppermute(head, axis, [((i + 1) % count, i) for i in range(ends)])  14.8 us
    all_to_all x2, local copies, waits for them, and re-layouts, on_device(): lax.all_to_all(across_strips, 'col', split_axis=2, concat_axis=1, tiled=T...  11.3 us
  transfers between devices with their start and end apart: 48, of which 24 were waited for; matrix products, arithmetic and copies ran while one was open for 9% of the time, Pallas kernels for 0%

commit v1 on v0

--- a/solution.py
+++ b/solution.py
@@ -92,7 +92,12 @@
 def on_device(term_images, blur_width, blur_coef, direct_coef, long_weight, long_gain, long_width):
     kernels = gauss_kernel(blur_width, REACH)
     tile_rows = term_images.shape[1]
-    strips = lax.all_to_all(term_images, "col", split_axis=1, concat_axis=2, tiled=True)
+    strips = jnp.concatenate(
+        lax.all_to_all(
+            jnp.stack(jnp.split(term_images, lax.axis_size("col"), axis=1)), "col", 0, 0
+        ),
+        axis=2,
+    )
     width_all = strips.shape[2]
     padded = jnp.pad(strips, ((0, 0), (0, 0), (REACH, REACH)))
     across_strips = taps_along(padded, kernels, 2, width_all)

time: 426 us -> 400 us (0.939)
  other arithmetic: 122 us -> 94 us
    add x1, other arithmetic: 46.7 us -> 18.8 us  [taps_along(): total + weights[:, tap_index] * lax.slice_in_dim(padded, tap_index, tap_i...]
    unnamed x11 -> x25, local copies, waits for them, and re-layouts: 32.2 us -> 39.5 us
    all_to_all x2 -> x0, local copies, waits for them, and re-layouts: 6.89 us -> none  [on_device(): lax.all_to_all(term_images, 'col', split_axis=1, concat_axis=2, tiled=True)]
  transfers between devices with their start and end apart: 48 -> 48, of which waited for: 24 -> 23; matrix products, arithmetic and copies ran while one was open for 9% -> 11% of each run, Pallas kernels for 0% -> 0%
where the time goes in v1:
time: 400 us; the launch traced here: 397 us
  starting transfers between devices  141 us (35%)
  other arithmetic  94 us (24%)
  waiting for transfers between devices  87.7 us (22%)
  local copies, waits for them, and re-layouts  71.7 us (18%)
    ppermute x23, waiting for transfers between devices, padded_2(): lax.ppermute(tail, axis, [(i, (i + 1) % count) for i in range(ends)])  70.3 us
    ppermute x23, starting transfers between devices, padded_2(): lax.ppermute(head, axis, [((i + 1) % count, i) for i in range(ends)])  68.1 us
    ppermute x23, starting transfers between devices, padded_2(): lax.ppermute(tail, axis, [(i, (i + 1) % count) for i in range(ends)])  60.7 us
    unnamed x25, local copies, waits for them, and re-layouts  39.5 us
    reduce_sum x1, other arithmetic, on_device(): jnp.sum(blur_coef[:, None, None] * blurred + direct_coef[:, None, None] *...  37.3 us
    add x1, other arithmetic, taps_along(): total + weights[:, tap_index] * lax.slice_in_dim(padded, tap_index, tap_i...  18.8 us
    ppermute x23, waiting for transfers between devices, padded_2(): lax.ppermute(head, axis, [((i + 1) % count, i) for i in range(ends)])  17.4 us
    all_to_all x2, local copies, waits for them, and re-layouts, on_device(): lax.all_to_all(across_strips, 'col', split_axis=2, concat_axis=1, tiled=T...  11.3 us
  transfers between devices with their start and end apart: 48, of which 23 were waited for; matrix products, arithmetic and copies ran while one was open for 11% of the time, Pallas kernels for 0%

profile of v1, /device:TPU:134, one launch (start us, length us, event | category | flops | bytes accessed | tf_op | source)
XLA Modules:
  0.0 397.1 jit_solution(16357556742267504729)
XLA Ops:
  0.0 2.0 fusion
  2.1 1.9 collective-permute-start.3
  4.0 2.4 collective-permute-start.2
  16.4 5.2 %collective-permute-start.5 = (f32[260,2]{1,0:T(8,128)S(1)}, f32[260,2]{1,0:T(8,128)S(1)}, u32[]{:S(2)}, u32[]{:S(2)}) collective-permute-start(f32[260,2]{1,0:T(8,128)S(1)} %get-tuple-element.8), channel_id=1, source_target_pairs={{1,0},{2,1},{3,2},{4,3},{5,4},{6,5},{7,6},{8,7},{9,8},{10,9},{11,1... | collective-permute-start | bytes 6248 | tf_op jit(solution)/shard_map/ppermute | solution.py:22
  21.6 1.9 collective-permute-start.4
  24.2 8.1 %all-to-all-start = ((f32[16,8,16,256]{3,2,1,0:T(8,128)}), f32[16,8,16,256]{3,2,1,0:T(8,128)}, u32[]{:S(2)}, u32[]{:S(2)}) async-start(f32[16,8,16,256]{3,2,1,0:T(8,128)} %bitcast_dynamic-update-slice_fusion), calls=%async_computation | async-start | bytes 4194304 | tf_op jit(solution)/shard_map/all_to_all | solution.py:96
  33.1 2.2 slice.1083
  35.3 3.2 collective-permute-start.7
  40.5 4.1 %collective-permute-done.6 = f32[2,128]{1,0:T(2,128)S(1)} collective-permute-done((f32[2,128]{1,0:T(2,128)S(1)}, f32[2,128]{1,0:T(2,128)S(1)}, u32[]{:S(2)}, u32[]{:S(2)}) %collective-permute-start.6) | collective-permute-done | bytes 1056 | tf_op jit(solution)/shard_map/ppermute | solution.py:20
  44.8 4.9 %collective-permute-start.9 = (f32[132,2]{1,0:T(8,128)S(1)}, f32[132,2]{1,0:T(8,128)S(1)}, u32[]{:S(2)}, u32[]{:S(2)}) collective-permute-start(f32[132,2]{1,0:T(8,128)S(1)} %get-tuple-element.22), channel_id=1, source_target_pairs={{1,0},{2,1},{3,2},{4,3},{5,4},{6,5},{7,6},{8,7},{9,8},{10,9},{11,1... | collective-permute-start | bytes 3176 | tf_op jit(solution)/shard_map/ppermute | solution.py:22
  51.6 9.5 %collective-permute-done.9 = f32[132,2]{1,0:T(8,128)S(1)} collective-permute-done((f32[132,2]{1,0:T(8,128)S(1)}, f32[132,2]{1,0:T(8,128)S(1)}, u32[]{:S(2)}, u32[]{:S(2)}) %collective-permute-start.9) | collective-permute-done | bytes 1088 | tf_op jit(solution)/shard_map/ppermute | solution.py:22
  62.9 1.9 collective-permute-start.11
  64.8 2.4 collective-permute-start.10
  67.4 3.5 collective-permute-done.10
  71.0 5.7 %collective-permute-start.13 = (f32[68,2]{1,0:T(8,128)S(1)}, f32[68,2]{1,0:T(8,128)S(1)}, u32[]{:S(2)}, u32[]{:S(2)}) collective-permute-start(f32[68,2]{1,0:T(8,128)S(1)} %get-tuple-element.34), channel_id=1, source_target_pairs={{1,0},{2,1},{3,2},{4,3},{5,4},{6,5},{7,6},{8,7},{9,8},{10,9},{11,1... | collective-permute-start | bytes 1640 | tf_op jit(solution)/shard_map/ppermute | solution.py:22
  76.7 1.9 collective-permute-start.12
  78.8 5.9 %collective-permute-done.12 = f32[68,2]{1,0:T(8,128)S(1)} collective-permute-done((f32[68,2]{1,0:T(8,128)S(1)}, f32[68,2]{1,0:T(8,128)S(1)}, u32[]{:S(2)}, u32[]{:S(2)}) %collective-permute-start.12) | collective-permute-done | bytes 576 | tf_op jit(solution)/shard_map/ppermute | solution.py:20
  85.1 1.9 collective-permute-start.15
  87.1 2.4 collective-permute-start.14
  90.1 3.0 collective-permute-done.14
  95.2 3.9 collective-permute-start.16
  99.1 3.8 collective-permute-done.16
  103.3 1.9 collective-permute-start.19
  105.2 2.4 collective-permute-start.18
  107.6 3.7 collective-permute-done.18
  113.3 3.9 collective-permute-start.20
  117.9 3.1 collective-permute-done.20
  121.3 1.9 collective-permute-start.23
  123.2 2.4 collective-permute-start.22
  126.2 3.1 collective-permute-done.22
  131.2 3.9 collective-permute-start.24
  135.9 3.1 collective-permute-done.24
  139.0 10.6 %fusion.192 = f32[8,24]{1,0:T(8,128)S(1)} fusion(f32[24,24]{1,0:T(8,128)S(1)} %pad_maximum_fusion.23, f32[]{:T(128)} %bitcast.74, f32[]{:T(128)} %bitcast.73, f32[]{:T(128)} %bitcast.72, f32[]{:T(128)} %bitcast.71, f32[]{:T(128)} %bitcast.70, f32[]{:T(128)} %bitcast.69, f32[]{:T(128)} %bitcast.68, f32[]{:T(128)} %bitcast.67, f32[]{:T(128)} %bitcast.66, ...), kind=kLoop, calls=%fused_computation.395 | loop fusion | flops 6336 | bytes 13892 | tf_op jit(solution)/shard_map/add | solution.py:75
  149.7 10.7 %multiply_add_fusion.1 = f32[8,8]{1,0:T(8,128)S(1)} fusion(f32[8,24]{1,0:T(8,128)S(1)} %fusion.192, f32[]{:T(128)} %bitcast.74, f32[]{:T(128)} %bitcast.73, f32[]{:T(128)} %bitcast.72, f32[]{:T(128)} %bitcast.71, f32[]{:T(128)} %bitcast.70, f32[]{:T(128)} %bitcast.69, f32[]{:T(128)} %bitcast.68, f32[]{:T(128)} %bitcast.67, f32[]{:T(128)} %bitcast.66, ...), kind=kLoop, calls=%fused_computation.428 | loop fusion | flops 2112 | bytes 4676 | tf_op jit(solution)/shard_map/add | solution.py:78
  162.3 2.4 collective-permute-start.26
  164.7 3.7 collective-permute-done.26
  170.4 3.9 collective-permute-start.28
  174.3 3.7 collective-permute-done.28
  180.8 2.4 collective-permute-start.30
  183.2 3.7 collective-permute-done.30
  189.0 3.9 collective-permute-start.32
  192.9 3.6 collective-permute-done.32
  199.2 4.9 %collective-permute-start.35 = (f32[1,32]{0,1:T(8,128)S(1)}, f32[1,32]{0,1:T(8,128)S(1)}, u32[]{:S(2)}, u32[]{:S(2)}) collective-permute-start(f32[1,32]{0,1:T(8,128)S(1)} %slice.1253), channel_id=1, source_target_pairs={{16,0},{32,16},{48,32},{64,48},{80,64},{96,80},{112,96},{128,112},... | collective-permute-start | bytes 392 | tf_op jit(solution)/shard_map/ppermute | solution.py:22
  207.5 4.1 %collective-permute-start.36 = (f32[34,1]{0,1:T(1,128)S(1)}, f32[34,1]{0,1:T(1,128)S(1)}, u32[]{:S(2)}, u32[]{:S(2)}) collective-permute-start(f32[34,1]{0,1:T(1,128)S(1)} %get-tuple-element.29), channel_id=1, source_target_pairs={{0,1},{1,2},{2,3},{3,4},{4,5},{5,6},{6,7},{7,8},{8,9},{9,10},{10,1... | collective-permute-start | bytes 416 | tf_op jit(solution)/shard_map/ppermute | solution.py:20
  211.6 3.4 collective-permute-done.36
  217.2 18.8 %multiply_add_fusion = f32[8,16,4096]{2,1,0:T(8,128)} fusion(f32[8,16,4096]{2,1,0:T(8,128)S(1)} %bitcast.181, f32[8]{0:T(128)S(1)} %get-tuple-element.48, f32[8]{0:T(128)S(1)} %get-tuple-element.49, f32[8]{0:T(128)S(1)} %get-tuple-element.50, f32[8]{0:T(128)S(1)} %get-tuple-element.51, f32[8]{0:T(128)S(1)} %get-tuple-element.52, ...), kind=kLoop, calls=%fused_computation.157 | loop fusion | flops 34078720 | bytes 4195360 | tf_op jit(solution)/shard_map/add | solution.py:86
  235.9 9.6 %copy.170 = f32[8,16,4096]{1,0,2:T(8,128)} copy(f32[8,16,4096]{2,1,0:T(8,128)} %multiply_add_fusion) | data formatting | bytes 4194304 | tf_op jit(solution)/shard_map/add | solution.py:86
  245.5 15.1 %reshape.242 = f32[16,1,32768]{2,1,0:T(1,128)} reshape(f32[4096,8,16]{2,1,0:T(8,128)} %bitcast.177) | data formatting | bytes 4194304
  260.6 4.5 %all-to-all-start.1 = ((f32[16,1,32768]{2,1,0:T(1,128)}), f32[16,1,32768]{2,1,0:T(1,128)}, u32[]{:S(2)}, u32[]{:S(2)}) async-start(f32[16,1,32768]{2,1,0:T(1,128)} %reshape.242), calls=%async_computation.1 | async-start | bytes 4194304 | tf_op jit(solution)/shard_map/all_to_all | solution.py:104
  265.4 3.5 collective-permute-start.39
  271.1 4.1 %collective-permute-done.38 = f32[1,64]{1,0:T(1,128)S(1)} collective-permute-done((f32[1,64]{1,0:T(1,128)S(1)}, f32[1,64]{1,0:T(1,128)S(1)}, u32[]{:S(2)}, u32[]{:S(2)}) %collective-permute-start.38) | collective-permute-done | bytes 288 | tf_op jit(solution)/shard_map/ppermute | solution.py:20
  275.4 4.5 %collective-permute-start.41 = (f32[66,1]{0,1:T(1,128)S(1)}, f32[66,1]{0,1:T(1,128)S(1)}, u32[]{:S(2)}, u32[]{:S(2)}) collective-permute-start(f32[66,1]{0,1:T(1,128)S(1)} %get-tuple-element.20), channel_id=1, source_target_pairs={{1,0},{2,1},{3,2},{4,3},{5,4},{6,5},{7,6},{8,7},{9,8},{10,9},{11,1... | collective-permute-start | bytes 800 | tf_op jit(solution)/shard_map/ppermute | solution.py:22
  281.8 6.6 %collective-permute-done.41 = f32[66,1]{0,1:T(1,128)S(1)} collective-permute-done((f32[66,1]{0,1:T(1,128)S(1)}, f32[66,1]{0,1:T(1,128)S(1)}, u32[]{:S(2)}, u32[]{:S(2)}) %collective-permute-start.41) | collective-permute-done | bytes 296 | tf_op jit(solution)/shard_map/ppermute | solution.py:22
  289.9 5.1 %collective-permute-start.43 = (f32[1,128]{0,1:T(8,128)S(1)}, f32[1,128]{0,1:T(8,128)S(1)}, u32[]{:S(2)}, u32[]{:S(2)}) collective-permute-start(f32[1,128]{0,1:T(8,128)S(1)} %slice.1255), channel_id=1, source_target_pairs={{16,0},{32,16},{48,32},{64,48},{80,64},{96,80},{112,96},{128,112},... | collective-permute-start | bytes 1544 | tf_op jit(solution)/shard_map/ppermute | solution.py:22
  297.2 4.1 %collective-permute-done.42 = f32[1,128]{1,0:T(1,128)S(1)} collective-permute-done((f32[1,128]{1,0:T(1,128)S(1)}, f32[1,128]{1,0:T(1,128)S(1)}, u32[]{:S(2)}, u32[]{:S(2)}) %collective-permute-start.42) | collective-permute-done | bytes 544 | tf_op jit(solution)/shard_map/ppermute | solution.py:20
  301.4 4.4 %collective-permute-start.45 = (f32[130,1]{0,1:T(1,128)S(1)}, f32[130,1]{0,1:T(1,128)S(1)}, u32[]{:S(2)}, u32[]{:S(2)}) collective-permute-start(f32[130,1]{0,1:T(1,128)S(1)} %get-tuple-element.14), channel_id=1, source_target_pairs={{1,0},{2,1},{3,2},{4,3},{5,4},{6,5},{7,6},{8,7},{9,8},{10,9},{11,1... | collective-permute-start | bytes 1568 | tf_op jit(solution)/shard_map/ppermute | solution.py:22
  305.8 2.1 collective-permute-start.44
  308.6 4.8 %collective-permute-done.44 = f32[130,1]{0,1:T(1,128)S(1)} collective-permute-done((f32[130,1]{0,1:T(1,128)S(1)}, f32[130,1]{0,1:T(1,128)S(1)}, u32[]{:S(2)}, u32[]{:S(2)}) %collective-permute-start.44) | collective-permute-done | bytes 552 | tf_op jit(solution)/shard_map/ppermute | solution.py:20
  314.5 8.6 %reduce.1 = f32[16,32768]{1,0:T(8,128)} reduce(f32[16,1,32768]{2,1,0:T(1,128)} %all-to-all-done.1, f32[]{:T(128)} %broadcast.217), dimensions={1}, to_apply=%all_to_all.17.reduce_sub_computation | reduce | bytes 4194308 | tf_op jit(solution)/shard_map/all_to_all | solution.py:104
  323.1 14.6 %reshape.243 = f32[4096,8,16]{2,1,0:T(8,128)} reshape(f32[16,32768]{1,0:T(8,128)} %reduce.1) | data formatting | bytes 4194304
  337.7 10.8 %copy.172 = f32[8,16,16,256]{3,2,1,0:T(8,128)} copy(f32[8,16,16,256]{2,0,3,1:T(8,128)} %bitcast.178) | data formatting | bytes 4194304 | tf_op jit(solution)/shard_map/all_to_all | solution.py:104
  351.5 2.7 collective-permute-start
  354.8 4.2 %collective-permute-done = f32[8,16,256]{2,1,0:T(8,128)S(1)} collective-permute-done((f32[8,16,256]{2,1,0:T(8,128)S(1)}, f32[8,16,256]{2,1,0:T(8,128)S(1)}, u32[]{:S(2)}, u32[]{:S(2)}) %collective-permute-start) | collective-permute-done | bytes 131104 | tf_op jit(solution)/shard_map/ppermute | solution.py:20
  359.0 37.3 %fusion.7 = f32[256,256]{1,0:T(8,128)S(1)} fusion(f32[8,16,256]{2,1,0:T(8,128)S(1)} %collective-permute-done.1, f32[8,16,256]{2,1,0:T(8,128)S(1)} %collective-permute-done, f32[8,256,256]{2,1,0:T(8,128)} %bitcast.180, f32[8,256,256]{2,1,0:T(8,128)S(1)} %copy-done, f32[8]{0:T(128)S(1)} %copy-done.1, f32[8]{0:T(128)S(1)} %get-tuple-element.48, ...), kind=kLoop, calls=%fused_computation.38 | loop fusion | flops 52887552 | bytes 4719712 | tf_op jit(solution)/shard_map/reduce_sum | solution.py:107
  (187 shorter events, 57.1 us)
Async XLA Ops:
  0.0 6.4 %copy-start = (f32[8,256,256]{2,1,0:T(8,128)S(1)}, f32[8,256,256]{2,1,0:T(8,128)}, u32[]{:S(2)}) copy-start(f32[8,256,256]{2,1,0:T(8,128)} %param.7) | copy-start | bytes 6291460
  2.1 14.2 %collective-permute-start.3 = (f32[2,256]{1,0:T(2,128)S(1)}, f32[2,256]{1,0:T(2,128)S(1)}, u32[]{:S(2)}, u32[]{:S(2)}) collective-permute-start(f32[2,256]{1,0:T(2,128)S(1)} %get-tuple-element.12), channel_id=1, source_target_pairs={{16,0},{32,16},{48,32},{64,48},{80,64},{96,80},{112,96},{128,112},... | collective-permute-start | bytes 6152 | tf_op jit(solution)/shard_map/ppermute | solution.py:22
  4.0 12.3 %collective-permute-start.2 = (f32[2,256]{1,0:T(2,128)S(1)}, f32[2,256]{1,0:T(2,128)S(1)}, u32[]{:S(2)}, u32[]{:S(2)}) collective-permute-start(f32[2,256]{1,0:T(2,128)S(1)} %get-tuple-element.11), channel_id=1, source_target_pairs={{0,16},{16,32},{32,48},{48,64},{64,80},{80,96},{96,112},{112,128},... | collective-permute-start | bytes 6152 | tf_op jit(solution)/shard_map/ppermute | solution.py:20
  16.4 15.9 %collective-permute-start.5 = (f32[260,2]{1,0:T(8,128)S(1)}, f32[260,2]{1,0:T(8,128)S(1)}, u32[]{:S(2)}, u32[]{:S(2)}) collective-permute-start(f32[260,2]{1,0:T(8,128)S(1)} %get-tuple-element.8), channel_id=1, source_target_pairs={{1,0},{2,1},{3,2},{4,3},{5,4},{6,5},{7,6},{8,7},{9,8},{10,9},{11,1... | collective-permute-start | bytes 6248 | tf_op jit(solution)/shard_map/ppermute | solution.py:22
  21.6 10.7 %collective-permute-start.4 = (f32[260,2]{1,0:T(8,128)S(1)}, f32[260,2]{1,0:T(8,128)S(1)}, u32[]{:S(2)}, u32[]{:S(2)}) collective-permute-start(f32[260,2]{1,0:T(8,128)S(1)} %get-tuple-element.7), channel_id=1, source_target_pairs={{0,1},{1,2},{2,3},{3,4},{4,5},{5,6},{6,7},{7,8},{8,9},{9,10},{10,1... | collective-permute-start | bytes 6248 | tf_op jit(solution)/shard_map/ppermute | solution.py:20
  24.2 191.2 %all-to-all-start = ((f32[16,8,16,256]{3,2,1,0:T(8,128)}), f32[16,8,16,256]{3,2,1,0:T(8,128)}, u32[]{:S(2)}, u32[]{:S(2)}) async-start(f32[16,8,16,256]{3,2,1,0:T(8,128)} %bitcast_dynamic-update-slice_fusion), calls=%async_computation | async-start | bytes 4194304 | tf_op jit(solution)/shard_map/all_to_all | solution.py:96
  32.5 8.0 %copy-start.3 = (f32[8]{0:T(128)S(1)}, f32[8]{0:T(128)}, u32[]{:S(2)}) copy-start(f32[8]{0:T(128)} %param.8) | copy-start | bytes 100
  35.3 5.2 %collective-permute-start.7 = (f32[2,128]{1,0:T(2,128)S(1)}, f32[2,128]{1,0:T(2,128)S(1)}, u32[]{:S(2)}, u32[]{:S(2)}) collective-permute-start(f32[2,128]{1,0:T(2,128)S(1)} %get-tuple-element.28), channel_id=1, source_target_pairs={{16,0},{32,16},{48,32},{64,48},{80,64},{96,80},{112,96},{128,112},... | collective-permute-start | bytes 3080 | tf_op jit(solution)/shard_map/ppermute | solution.py:22
  38.6 6.1 %collective-permute-start.6 = (f32[2,128]{1,0:T(2,128)S(1)}, f32[2,128]{1,0:T(2,128)S(1)}, u32[]{:S(2)}, u32[]{:S(2)}) collective-permute-start(f32[2,128]{1,0:T(2,128)S(1)} %get-tuple-element.27), channel_id=1, source_target_pairs={{0,16},{16,32},{32,48},{48,64},{64,80},{80,96},{96,112},{112,128},... | collective-permute-start | bytes 3080 | tf_op jit(solution)/shard_map/ppermute | solution.py:20
  44.8 16.3 %collective-permute-start.9 = (f32[132,2]{1,0:T(8,128)S(1)}, f32[132,2]{1,0:T(8,128)S(1)}, u32[]{:S(2)}, u32[]{:S(2)}) collective-permute-start(f32[132,2]{1,0:T(8,128)S(1)} %get-tuple-element.22), channel_id=1, source_target_pairs={{1,0},{2,1},{3,2},{4,3},{5,4},{6,5},{7,6},{8,7},{9,8},{10,9},{11,1... | collective-permute-start | bytes 3176 | tf_op jit(solution)/shard_map/ppermute | solution.py:22
  49.6 12.3 %collective-permute-start.8 = (f32[132,2]{1,0:T(8,128)S(1)}, f32[132,2]{1,0:T(8,128)S(1)}, u32[]{:S(2)}, u32[]{:S(2)}) collective-permute-start(f32[132,2]{1,0:T(8,128)S(1)} %get-tuple-element.21), channel_id=1, source_target_pairs={{0,1},{1,2},{2,3},{3,4},{4,5},{5,6},{6,7},{7,8},{8,9},{9,10},{10,1... | collective-permute-start | bytes 3176 | tf_op jit(solution)/shard_map/ppermute | solution.py:20
  62.9 4.5 %collective-permute-start.11 = (f32[2,64]{1,0:T(2,128)S(1)}, f32[2,64]{1,0:T(2,128)S(1)}, u32[]{:S(2)}, u32[]{:S(2)}) collective-permute-start(f32[2,64]{1,0:T(2,128)S(1)} %get-tuple-element.40), channel_id=1, source_target_pairs={{16,0},{32,16},{48,32},{64,48},{80,64},{96,80},{112,96},{128,112},... | collective-permute-start | bytes 1544 | tf_op jit(solution)/shard_map/ppermute | solution.py:22
  64.8 6.1 %collective-permute-start.10 = (f32[2,64]{1,0:T(2,128)S(1)}, f32[2,64]{1,0:T(2,128)S(1)}, u32[]{:S(2)}, u32[]{:S(2)}) collective-permute-start(f32[2,64]{1,0:T(2,128)S(1)} %get-tuple-element.39), channel_id=1, source_target_pairs={{0,16},{16,32},{32,48},{48,64},{64,80},{80,96},{96,112},{112,128},... | collective-permute-start | bytes 1544 | tf_op jit(solution)/shard_map/ppermute | solution.py:20
  71.0 7.7 %collective-permute-start.13 = (f32[68,2]{1,0:T(8,128)S(1)}, f32[68,2]{1,0:T(8,128)S(1)}, u32[]{:S(2)}, u32[]{:S(2)}) collective-permute-start(f32[68,2]{1,0:T(8,128)S(1)} %get-tuple-element.34), channel_id=1, source_target_pairs={{1,0},{2,1},{3,2},{4,3},{5,4},{6,5},{7,6},{8,7},{9,8},{10,9},{11,1... | collective-permute-start | bytes 1640 | tf_op jit(solution)/shard_map/ppermute | solution.py:22
  76.7 8.0 %collective-permute-start.12 = (f32[68,2]{1,0:T(8,128)S(1)}, f32[68,2]{1,0:T(8,128)S(1)}, u32[]{:S(2)}, u32[]{:S(2)}) collective-permute-start(f32[68,2]{1,0:T(8,128)S(1)} %get-tuple-element.33), channel_id=1, source_target_pairs={{0,1},{1,2},{2,3},{3,4},{4,5},{5,6},{6,7},{7,8},{8,9},{9,10},{10,1... | collective-permute-start | bytes 1640 | tf_op jit(solution)/shard_map/ppermute | solution.py:20
  85.1 5.0 %collective-permute-start.15 = (f32[2,32]{1,0:T(2,128)S(1)}, f32[2,32]{1,0:T(2,128)S(1)}, u32[]{:S(2)}, u32[]{:S(2)}) collective-permute-start(f32[2,32]{1,0:T(2,128)S(1)} %get-tuple-element.83), channel_id=1, source_target_pairs={{16,0},{32,16},{48,32},{64,48},{80,64},{96,80},{112,96},{128,112},... | collective-permute-start | bytes 776 | tf_op jit(solution)/shard_map/ppermute | solution.py:22
  87.1 6.1 %collective-permute-start.14 = (f32[2,32]{1,0:T(2,128)S(1)}, f32[2,32]{1,0:T(2,128)S(1)}, u32[]{:S(2)}, u32[]{:S(2)}) collective-permute-start(f32[2,32]{1,0:T(2,128)S(1)} %get-tuple-element.82), channel_id=1, source_target_pairs={{0,16},{16,32},{32,48},{48,64},{64,80},{80,96},{96,112},{112,128},... | collective-permute-start | bytes 776 | tf_op jit(solution)/shard_map/ppermute | solution.py:20
  93.2 5.9 %collective-permute-start.17 = (f32[36,2]{1,0:T(8,128)S(1)}, f32[36,2]{1,0:T(8,128)S(1)}, u32[]{:S(2)}, u32[]{:S(2)}) collective-permute-start(f32[36,2]{1,0:T(8,128)S(1)} %get-tuple-element.46), channel_id=1, source_target_pairs={{1,0},{2,1},{3,2},{4,3},{5,4},{6,5},{7,6},{8,7},{9,8},{10,9},{11,1... | collective-permute-start | bytes 872 | tf_op jit(solution)/shard_map/ppermute | solution.py:22
  95.2 7.8 %collective-permute-start.16 = (f32[36,2]{1,0:T(8,128)S(1)}, f32[36,2]{1,0:T(8,128)S(1)}, u32[]{:S(2)}, u32[]{:S(2)}) collective-permute-start(f32[36,2]{1,0:T(8,128)S(1)} %get-tuple-element.45), channel_id=1, source_target_pairs={{0,1},{1,2},{2,3},{3,4},{4,5},{5,6},{6,7},{7,8},{8,9},{9,10},{10,1... | collective-permute-start | bytes 872 | tf_op jit(solution)/shard_map/ppermute | solution.py:20
  103.3 4.4 %collective-permute-start.19 = (f32[2,16]{1,0:T(2,128)S(1)}, f32[2,16]{1,0:T(2,128)S(1)}, u32[]{:S(2)}, u32[]{:S(2)}) collective-permute-start(f32[2,16]{1,0:T(2,128)S(1)} %get-tuple-element.97), channel_id=1, source_target_pairs={{16,0},{32,16},{48,32},{64,48},{80,64},{96,80},{112,96},{128,112},... | collective-permute-start | bytes 392 | tf_op jit(solution)/shard_map/ppermute | solution.py:22
  105.2 6.1 %collective-permute-start.18 = (f32[2,16]{1,0:T(2,128)S(1)}, f32[2,16]{1,0:T(2,128)S(1)}, u32[]{:S(2)}, u32[]{:S(2)}) collective-permute-start(f32[2,16]{1,0:T(2,128)S(1)} %get-tuple-element.96), channel_id=1, source_target_pairs={{0,16},{16,32},{32,48},{48,64},{64,80},{80,96},{96,112},{112,128},... | collective-permute-start | bytes 392 | tf_op jit(solution)/shard_map/ppermute | solution.py:20
  111.4 6.5 %collective-permute-start.21 = (f32[20,2]{1,0:T(8,128)S(1)}, f32[20,2]{1,0:T(8,128)S(1)}, u32[]{:S(2)}, u32[]{:S(2)}) collective-permute-start(f32[20,2]{1,0:T(8,128)S(1)} %get-tuple-element.87), channel_id=1, source_target_pairs={{1,0},{2,1},{3,2},{4,3},{5,4},{6,5},{7,6},{8,7},{9,8},{10,9},{11,1... | collective-permute-start | bytes 488 | tf_op jit(solution)/shard_map/ppermute | solution.py:22
  113.3 7.7 %collective-permute-start.20 = (f32[20,2]{1,0:T(8,128)S(1)}, f32[20,2]{1,0:T(8,128)S(1)}, u32[]{:S(2)}, u32[]{:S(2)}) collective-permute-start(f32[20,2]{1,0:T(8,128)S(1)} %get-tuple-element.86), channel_id=1, source_target_pairs={{0,1},{1,2},{2,3},{3,4},{4,5},{5,6},{6,7},{7,8},{8,9},{9,10},{10,1... | collective-permute-start | bytes 488 | tf_op jit(solution)/shard_map/ppermute | solution.py:20
  121.3 4.9 %collective-permute-start.23 = (f32[8,8]{1,0:T(8,128)S(1)}, f32[8,8]{1,0:T(8,128)S(1)}, u32[]{:S(2)}, u32[]{:S(2)}) collective-permute-start(f32[8,8]{1,0:T(8,128)S(1)} %slice.1143), channel_id=1, source_target_pairs={{16,0},{32,16},{48,32},{64,48},{80,64},{96,80},{112,96},{128,112},... | collective-permute-start | bytes 776 | tf_op jit(solution)/shard_map/ppermute | solution.py:22
  123.2 6.1 %collective-permute-start.22 = (f32[8,8]{1,0:T(8,128)S(1)}, f32[8,8]{1,0:T(8,128)S(1)}, u32[]{:S(2)}, u32[]{:S(2)}) collective-permute-start(f32[8,8]{1,0:T(8,128)S(1)} %slice.1143), channel_id=1, source_target_pairs={{0,16},{16,32},{32,48},{48,64},{64,80},{80,96},{96,112},{112,128},... | collective-permute-start | bytes 776 | tf_op jit(solution)/shard_map/ppermute | solution.py:20
  129.3 6.6 %collective-permute-start.25 = (f32[24,8]{1,0:T(8,128)S(1)}, f32[24,8]{1,0:T(8,128)S(1)}, u32[]{:S(2)}, u32[]{:S(2)}) collective-permute-start(f32[24,8]{1,0:T(8,128)S(1)} %pad_maximum_fusion.22), channel_id=1, source_target_pairs={{1,0},{2,1},{3,2},{4,3},{5,4},{6,5},{7,6},{8,7},{9,8},{10,9},{11,1... | collective-permute-start | bytes 2312 | tf_op jit(solution)/shard_map/ppermute | solution.py:22
  131.2 7.7 %collective-permute-start.24 = (f32[24,8]{1,0:T(8,128)S(1)}, f32[24,8]{1,0:T(8,128)S(1)}, u32[]{:S(2)}, u32[]{:S(2)}) collective-permute-start(f32[24,8]{1,0:T(8,128)S(1)} %pad_maximum_fusion.22), channel_id=1, source_target_pairs={{0,1},{1,2},{2,3},{3,4},{4,5},{5,6},{6,7},{7,8},{8,9},{9,10},{10,1... | collective-permute-start | bytes 2312 | tf_op jit(solution)/shard_map/ppermute | solution.py:20
  160.4 4.3 %collective-permute-start.27 = (f32[1,8]{1,0:T(1,128)S(1)}, f32[1,8]{1,0:T(1,128)S(1)}, u32[]{:S(2)}, u32[]{:S(2)}) collective-permute-start(f32[1,8]{1,0:T(1,128)S(1)} %get-tuple-element.99), channel_id=1, source_target_pairs={{16,0},{32,16},{48,32},{64,48},{80,64},{96,80},{112,96},{128,112},... | collective-permute-start | bytes 104 | tf_op jit(solution)/shard_map/ppermute | solution.py:22
  162.3 6.1 %collective-permute-start.26 = (f32[1,8]{1,0:T(1,128)S(1)}, f32[1,8]{1,0:T(1,128)S(1)}, u32[]{:S(2)}, u32[]{:S(2)}) collective-permute-start(f32[1,8]{1,0:T(1,128)S(1)} %get-tuple-element.98), channel_id=1, source_target_pairs={{0,16},{16,32},{32,48},{48,64},{64,80},{80,96},{96,112},{112,128},... | collective-permute-start | bytes 104 | tf_op jit(solution)/shard_map/ppermute | solution.py:20
  168.5 5.9 %collective-permute-start.29 = (f32[10,1]{1,0:T(8,128)S(1)}, f32[10,1]{1,0:T(8,128)S(1)}, u32[]{:S(2)}, u32[]{:S(2)}) collective-permute-start(f32[10,1]{1,0:T(8,128)S(1)} %get-tuple-element.95), channel_id=1, source_target_pairs={{1,0},{2,1},{3,2},{4,3},{5,4},{6,5},{7,6},{8,7},{9,8},{10,9},{11,1... | collective-permute-start | bytes 128 | tf_op jit(solution)/shard_map/ppermute | solution.py:22
  170.4 7.7 %collective-permute-start.28 = (f32[10,1]{1,0:T(8,128)S(1)}, f32[10,1]{1,0:T(8,128)S(1)}, u32[]{:S(2)}, u32[]{:S(2)}) collective-permute-start(f32[10,1]{1,0:T(8,128)S(1)} %get-tuple-element.94), channel_id=1, source_target_pairs={{0,1},{1,2},{2,3},{3,4},{4,5},{5,6},{6,7},{7,8},{8,9},{9,10},{10,1... | collective-permute-start | bytes 128 | tf_op jit(solution)/shard_map/ppermute | solution.py:20
  178.7 8.3 %collective-permute-start.31 = (f32[1,16]{0,1:T(8,128)S(1)}, f32[1,16]{0,1:T(8,128)S(1)}, u32[]{:S(2)}, u32[]{:S(2)}) collective-permute-start(f32[1,16]{0,1:T(8,128)S(1)} %slice.1252), channel_id=1, source_target_pairs={{16,0},{32,16},{48,32},{64,48},{80,64},{96,80},{112,96},{128,112},... | collective-permute-start | bytes 200 | tf_op jit(solution)/shard_map/ppermute | solution.py:22
  180.8 6.1 %collective-permute-start.30 = (f32[1,16]{1,0:T(1,128)S(1)}, f32[1,16]{1,0:T(1,128)S(1)}, u32[]{:S(2)}, u32[]{:S(2)}) collective-permute-start(f32[1,16]{1,0:T(1,128)S(1)} %slice.1205), channel_id=1, source_target_pairs={{0,16},{16,32},{32,48},{48,64},{64,80},{80,96},{96,112},{112,128},... | collective-permute-start | bytes 200 | tf_op jit(solution)/shard_map/ppermute | solution.py:20
  187.1 5.9 %collective-permute-start.33 = (f32[18,1]{0,1:T(1,128)S(1)}, f32[18,1]{0,1:T(1,128)S(1)}, u32[]{:S(2)}, u32[]{:S(2)}) collective-permute-start(f32[18,1]{0,1:T(1,128)S(1)} %get-tuple-element.42), channel_id=1, source_target_pairs={{1,0},{2,1},{3,2},{4,3},{5,4},{6,5},{7,6},{8,7},{9,8},{10,9},{11,1... | collective-permute-start | bytes 224 | tf_op jit(solution)/shard_map/ppermute | solution.py:22
  189.0 7.6 %collective-permute-start.32 = (f32[18,1]{0,1:T(1,128)S(1)}, f32[18,1]{0,1:T(1,128)S(1)}, u32[]{:S(2)}, u32[]{:S(2)}) collective-permute-start(f32[18,1]{0,1:T(1,128)S(1)} %get-tuple-element.41), channel_id=1, source_target_pairs={{0,1},{1,2},{2,3},{3,4},{4,5},{5,6},{6,7},{7,8},{8,9},{9,10},{10,1... | collective-permute-start | bytes 224 | tf_op jit(solution)/shard_map/ppermute | solution.py:20
  197.3 6.9 %collective-permute-start.34 = (f32[1,32]{1,0:T(1,128)S(1)}, f32[1,32]{1,0:T(1,128)S(1)}, u32[]{:S(2)}, u32[]{:S(2)}) collective-permute-start(f32[1,32]{1,0:T(1,128)S(1)} %slice.1217), channel_id=1, source_target_pairs={{0,16},{16,32},{32,48},{48,64},{64,80},{80,96},{96,112},{112,128},... | collective-permute-start | bytes 392 | tf_op jit(solution)/shard_map/ppermute | solution.py:20
  199.2 6.3 %collective-permute-start.35 = (f32[1,32]{0,1:T(8,128)S(1)}, f32[1,32]{0,1:T(8,128)S(1)}, u32[]{:S(2)}, u32[]{:S(2)}) collective-permute-start(f32[1,32]{0,1:T(8,128)S(1)} %slice.1253), channel_id=1, source_target_pairs={{16,0},{32,16},{48,32},{64,48},{80,64},{96,80},{112,96},{128,112},... | collective-permute-start | bytes 392 | tf_op jit(solution)/shard_map/ppermute | solution.py:22
  205.6 6.0 %collective-permute-start.37 = (f32[34,1]{0,1:T(1,128)S(1)}, f32[34,1]{0,1:T(1,128)S(1)}, u32[]{:S(2)}, u32[]{:S(2)}) collective-permute-start(f32[34,1]{0,1:T(1,128)S(1)} %get-tuple-element.30), channel_id=1, source_target_pairs={{1,0},{2,1},{3,2},{4,3},{5,4},{6,5},{7,6},{8,7},{9,8},{10,9},{11,1... | collective-permute-start | bytes 416 | tf_op jit(solution)/shard_map/ppermute | solution.py:22
  207.5 7.6 %collective-permute-start.36 = (f32[34,1]{0,1:T(1,128)S(1)}, f32[34,1]{0,1:T(1,128)S(1)}, u32[]{:S(2)}, u32[]{:S(2)}) collective-permute-start(f32[34,1]{0,1:T(1,128)S(1)} %get-tuple-element.29), channel_id=1, source_target_pairs={{0,1},{1,2},{2,3},{3,4},{4,5},{5,6},{6,7},{7,8},{8,9},{9,10},{10,1... | collective-permute-start | bytes 416 | tf_op jit(solution)/shard_map/ppermute | solution.py:20
  260.6 53.4 %all-to-all-start.1 = ((f32[16,1,32768]{2,1,0:T(1,128)}), f32[16,1,32768]{2,1,0:T(1,128)}, u32[]{:S(2)}, u32[]{:S(2)}) async-start(f32[16,1,32768]{2,1,0:T(1,128)} %reshape.242), calls=%async_computation.1 | async-start | bytes 4194304 | tf_op jit(solution)/shard_map/all_to_all | solution.py:104
  265.4 9.9 %collective-permute-start.39 = (f32[1,64]{0,1:T(8,128)S(1)}, f32[1,64]{0,1:T(8,128)S(1)}, u32[]{:S(2)}, u32[]{:S(2)}) collective-permute-start(f32[1,64]{0,1:T(8,128)S(1)} %slice.1254), channel_id=1, source_target_pairs={{16,0},{32,16},{48,32},{64,48},{80,64},{96,80},{112,96},{128,112},... | collective-permute-start | bytes 776 | tf_op jit(solution)/shard_map/ppermute | solution.py:22
  269.1 6.1 %collective-permute-start.38 = (f32[1,64]{1,0:T(1,128)S(1)}, f32[1,64]{1,0:T(1,128)S(1)}, u32[]{:S(2)}, u32[]{:S(2)}) collective-permute-start(f32[1,64]{1,0:T(1,128)S(1)} %slice.1229), channel_id=1, source_target_pairs={{0,16},{16,32},{32,48},{48,64},{64,80},{80,96},{96,112},{112,128},... | collective-permute-start | bytes 776 | tf_op jit(solution)/shard_map/ppermute | solution.py:20
  275.4 13.0 %collective-permute-start.41 = (f32[66,1]{0,1:T(1,128)S(1)}, f32[66,1]{0,1:T(1,128)S(1)}, u32[]{:S(2)}, u32[]{:S(2)}) collective-permute-start(f32[66,1]{0,1:T(1,128)S(1)} %get-tuple-element.20), channel_id=1, source_target_pairs={{1,0},{2,1},{3,2},{4,3},{5,4},{6,5},{7,6},{8,7},{9,8},{10,9},{11,1... | collective-permute-start | bytes 800 | tf_op jit(solution)/shard_map/ppermute | solution.py:22
  279.9 9.4 %collective-permute-start.40 = (f32[66,1]{0,1:T(1,128)S(1)}, f32[66,1]{0,1:T(1,128)S(1)}, u32[]{:S(2)}, u32[]{:S(2)}) collective-permute-start(f32[66,1]{0,1:T(1,128)S(1)} %get-tuple-element.19), channel_id=1, source_target_pairs={{0,1},{1,2},{2,3},{3,4},{4,5},{5,6},{6,7},{7,8},{8,9},{9,10},{10,1... | collective-permute-start | bytes 800 | tf_op jit(solution)/shard_map/ppermute | solution.py:20
  289.9 11.5 %collective-permute-start.43 = (f32[1,128]{0,1:T(8,128)S(1)}, f32[1,128]{0,1:T(8,128)S(1)}, u32[]{:S(2)}, u32[]{:S(2)}) collective-permute-start(f32[1,128]{0,1:T(8,128)S(1)} %slice.1255), channel_id=1, source_target_pairs={{16,0},{32,16},{48,32},{64,48},{80,64},{96,80},{112,96},{128,112},... | collective-permute-start | bytes 1544 | tf_op jit(solution)/shard_map/ppermute | solution.py:22
  295.2 6.1 %collective-permute-start.42 = (f32[1,128]{1,0:T(1,128)S(1)}, f32[1,128]{1,0:T(1,128)S(1)}, u32[]{:S(2)}, u32[]{:S(2)}) collective-permute-start(f32[1,128]{1,0:T(1,128)S(1)} %slice.1241), channel_id=1, source_target_pairs={{0,16},{16,32},{32,48},{48,64},{64,80},{80,96},{96,112},{112,128},... | collective-permute-start | bytes 1544 | tf_op jit(solution)/shard_map/ppermute | solution.py:20
  301.4 7.2 %collective-permute-start.45 = (f32[130,1]{0,1:T(1,128)S(1)}, f32[130,1]{0,1:T(1,128)S(1)}, u32[]{:S(2)}, u32[]{:S(2)}) collective-permute-start(f32[130,1]{0,1:T(1,128)S(1)} %get-tuple-element.14), channel_id=1, source_target_pairs={{1,0},{2,1},{3,2},{4,3},{5,4},{6,5},{7,6},{8,7},{9,8},{10,9},{11,1... | collective-permute-start | bytes 1568 | tf_op jit(solution)/shard_map/ppermute | solution.py:22
  305.8 7.6 %collective-permute-start.44 = (f32[130,1]{0,1:T(1,128)S(1)}, f32[130,1]{0,1:T(1,128)S(1)}, u32[]{:S(2)}, u32[]{:S(2)}) collective-permute-start(f32[130,1]{0,1:T(1,128)S(1)} %get-tuple-element.13), channel_id=1, source_target_pairs={{0,1},{1,2},{2,3},{3,4},{4,5},{5,6},{6,7},{7,8},{8,9},{9,10},{10,1... | collective-permute-start | bytes 1568 | tf_op jit(solution)/shard_map/ppermute | solution.py:20
  348.5 10.4 %copy-start.1 = (f32[8]{0:T(128)S(1)}, f32[8]{0:T(128)}, u32[]{:S(2)}) copy-start(f32[8]{0:T(128)} %param.10) | copy-start | bytes 100
  348.5 10.4 %copy-start.2 = (f32[8]{0:T(128)S(1)}, f32[8]{0:T(128)}, u32[]{:S(2)}) copy-start(f32[8]{0:T(128)} %param.9) | copy-start | bytes 100
  349.6 5.3 %collective-permute-start.1 = (f32[8,16,256]{2,1,0:T(8,128)S(1)}, f32[8,16,256]{2,1,0:T(8,128)S(1)}, u32[]{:S(2)}, u32[]{:S(2)}) collective-permute-start(f32[8,16,256]{2,1,0:T(8,128)S(1)} %get-tuple-element.6), channel_id=1, source_target_pairs={{16,0},{32,16},{48,32},{64,48},{80,64},{96,80},{112,96},{128,112},... | collective-permute-start | bytes 393224 | tf_op jit(solution)/shard_map/ppermute | solution.py:22
  351.5 7.5 %collective-permute-start = (f32[8,16,256]{2,1,0:T(8,128)S(1)}, f32[8,16,256]{2,1,0:T(8,128)S(1)}, u32[]{:S(2)}, u32[]{:S(2)}) collective-permute-start(f32[8,16,256]{2,1,0:T(8,128)S(1)} %get-tuple-element.5), channel_id=1, source_target_pairs={{0,16},{16,32},{32,48},{48,64},{64,80},{80,96},{96,112},{112,128},... | collective-permute-start | bytes 393224 | tf_op jit(solution)/shard_map/ppermute | solution.py:20
